TPU v7x, 128 devices: a whole 4x4x4 slice. The times are simulated.
128 devices in a mesh: section: 4 (over y_hi, core), frame: 32 (over y_lo, x, z).
Axes of the slice: x: 4, y: 4 (y_hi: 2, y_lo: 2; y = y_hi * 2 + y_lo), z: 4, core: 2. Of those that a mesh axis runs over, the one named last changes fastest.
Arguments:
- newcomer_groups: bfloat16 [1, 8192, 1536], P(None, 'frame'), may hold values from -6 to 6
- pending_inputs: bfloat16 [4, 8192, 1536], P('section', 'frame'), may hold values from -6 to 6
- speaker_clip_ids: int32 [5, 8192], P(None, 'frame'), may hold values from 0 to 63, never falling along the last dimension, each value on 1 to 256 neighbouring positions
- selfattend_scaling: float32 [4, 1536], P('section'), may hold values from 0.1 to 1.9
- triple_projection_matrix: bfloat16 [4, 1536, 4608], P('section', 'frame'), may hold values from -1 to 1
- selfattend_final_matrix: bfloat16 [4, 1536, 1536], P('section', 'frame'), may hold values from -0.15625 to 0.15625
- depthwise_scaling: float32 [4, 1536], P('section'), may hold values from 0.1 to 1.9
- sigmoid_expand_matrix: bfloat16 [4, 1536, 3072], P('section', 'frame'), may hold values from -0.15625 to 0.15625
- filter_taps: float32 [4, 31, 1536], P('section'), may hold values from -1 to 1
- combine_channel_matrix: bfloat16 [4, 1536, 1536], P('section', 'frame'), may hold values from -0.15625 to 0.15625
Outputs:
- section_out: bfloat16 [2, 4, 8192, 1536], P(None, 'section', 'frame')
Inputs may be any that keep to these rules, and one draw needn't show every extreme that they name: `speaker_clip_ids`: in every row the ids never fall along frames; every utterance has 1 to 256 frames, and one utterance of each row has exactly 256.
All inputs are finite; a program needn't handle non-finite values.
Results may differ from a plain program's by a relative error of at most 0.008.
Values may be sent and summed in bfloat16 or wider, within the bound.
A program may use at most 192 MiB of HBM per device.

v0:
```python
import jax
import jax.numpy as jnp
from jax import lax
from jax.sharding import PartitionSpec as P

HEADS = 24
KERNEL = 31
EPS = 1e-05


def extended(block, sides, width):
    for axis, dim in sides:
        count = lax.axis_size(axis)
        forward = [(i, i + 1) for i in range(count - 1)]
        backward = [(target, source) for source, target in forward]
        low = lax.ppermute(
            lax.slice_in_dim(block, block.shape[dim] - width, None, axis=dim), axis, forward
        )
        high = lax.ppermute(lax.slice_in_dim(block, 0, width, axis=dim), axis, backward)
        block = jnp.concatenate([low, block, high], axis=dim)
    return block


def shifted(value, axis, steps):
    count = lax.axis_size(axis)
    leading, last = (max(0, -steps), min(count, count - steps))
    return lax.ppermute(value, axis, [(source, source + steps) for source in range(leading, last)])


def layer_norm(sample_lines, gain):
    mean = jnp.mean(sample_lines, axis=-1, keepdims=True)
    centred = sample_lines - mean
    spread = jnp.mean(centred * centred, axis=-1, keepdims=True)
    return centred * lax.rsqrt(spread + EPS) * gain


def attend(query, wide_keys, wide_values, seg_wide, seg_own):
    sample_lines, feature_count = query.shape
    head_dim = feature_count // HEADS
    shaped_q = query.reshape(sample_lines, HEADS, head_dim)
    shaped_k = wide_keys.reshape(wide_keys.shape[0], HEADS, head_dim)
    shaped_v = wide_values.reshape(wide_values.shape[0], HEADS, head_dim)
    scores = jnp.einsum("qhd,khd->hqk", shaped_q, shaped_k, preferred_element_type=jnp.float32)
    allowed = (seg_own[:, None] == seg_wide[None, :])[None]
    scores = jnp.where(allowed, scores, -1e30)
    top = jnp.max(scores, axis=-1, keepdims=True)
    expd = jnp.exp(scores - top)
    probs = (expd / jnp.sum(expd, axis=-1, keepdims=True)).astype(jnp.bfloat16)
    context = jnp.einsum("hqk,khd->qhd", probs, shaped_v, preferred_element_type=jnp.float32)
    return context.astype(jnp.bfloat16).reshape(sample_lines, feature_count)


def depthwise(wide_glu, seg_conv, seg_own, taps):
    sample_lines = seg_own.shape[0]
    total = jnp.zeros((sample_lines, wide_glu.shape[1]), jnp.float32)
    for tap in range(taps.shape[0]):
        same = (seg_conv[tap : tap + sample_lines] == seg_own)[:, None]
        total = total + jnp.where(
            same, wide_glu[tap : tap + sample_lines].astype(jnp.float32) * taps[tap], 0.0
        )
    return total


def on_device(
    newcomer_groups,
    pending_inputs,
    speaker_clip_ids,
    selfattend_scaling,
    triple_projection_matrix,
    selfattend_final_matrix,
    depthwise_scaling,
    sigmoid_expand_matrix,
    filter_taps,
    combine_channel_matrix,
):
    sample_lines = pending_inputs.shape[1]
    feature_count = pending_inputs.shape[2]
    half = KERNEL // 2
    sections = lax.axis_size("section")
    section = lax.axis_index("section")
    ticks = newcomer_groups.shape[0] + 1
    seg_all = extended(speaker_clip_ids + 1, (("frame", 1),), sample_lines)
    full_qkv, full_out, full_glu, full_mix = (
        lax.all_gather(triple_projection_matrix[0], "frame", axis=0, tiled=True),
        lax.all_gather(selfattend_final_matrix[0], "frame", axis=0, tiled=True),
        lax.all_gather(sigmoid_expand_matrix[0], "frame", axis=0, tiled=True),
        lax.all_gather(combine_channel_matrix[0], "frame", axis=0, tiled=True),
    )
    present_activity = pending_inputs[0]
    made_all = []
    for tick in range(ticks):
        batch_index = sections - 1 - section + tick
        seg_wide = lax.dynamic_index_in_dim(seg_all, batch_index, 0, keepdims=False)
        seg_own = seg_wide[sample_lines : 2 * sample_lines]
        resid = present_activity.astype(jnp.float32)
        normed = layer_norm(resid, selfattend_scaling[0]).astype(jnp.bfloat16)
        projected = jnp.dot(normed, full_qkv, preferred_element_type=jnp.float32)
        query = (projected[:, :feature_count] * (feature_count // HEADS) ** (-0.5)).astype(
            jnp.bfloat16
        )
        keys = projected[:, feature_count : 2 * feature_count].astype(jnp.bfloat16)
        values = projected[:, 2 * feature_count :].astype(jnp.bfloat16)
        wide_keys, wide_values = (
            extended(keys, (("frame", 0),), sample_lines),
            extended(values, (("frame", 0),), sample_lines),
        )
        context = attend(query, wide_keys, wide_values, seg_wide, seg_own)
        resid = resid + jnp.dot(context, full_out, preferred_element_type=jnp.float32)
        conv_in = layer_norm(resid, depthwise_scaling[0]).astype(jnp.bfloat16)
        doubled = jnp.dot(conv_in, full_glu, preferred_element_type=jnp.float32)
        glu = (doubled[:, :feature_count] * jax.nn.sigmoid(doubled[:, feature_count:])).astype(
            jnp.bfloat16
        )
        wide_glu = extended(glu, (("frame", 0),), half)
        depth = depthwise(
            wide_glu,
            seg_wide[sample_lines - half : 2 * sample_lines + half],
            seg_own,
            filter_taps[0],
        )
        act = (depth * jax.nn.sigmoid(depth)).astype(jnp.bfloat16)
        resid = resid + jnp.dot(act, full_mix, preferred_element_type=jnp.float32)
        made = resid.astype(jnp.bfloat16)
        made_all.append(made)
        if tick + 1 < ticks:
            arrived = shifted(made, "section", 1)
            present_activity = jnp.where(section == 0, newcomer_groups[tick], arrived)
    return jnp.stack(made_all)[:, None]


def solution(mesh):
    in_specs = (
        P(None, "frame", None),
        P("section", "frame", None),
        P(None, "frame"),
        P("section", None),
        P("section", "frame", None),
        P("section", "frame", None),
        P("section", None),
        P("section", "frame", None),
        P("section", None, None),
        P("section", "frame", None),
    )
    out_specs = P(None, "section", "frame", None)
    return jax.shard_map(
        on_device, mesh=mesh, in_specs=in_specs, out_specs=out_specs, check_vma=False
    )
```

profile of v0, /device:TPU:118, one launch (start us, length us, event | category | flops | bytes accessed | tf_op | source)
XLA Modules:
  0.0 833.5 jit_solution(4557215190937780094)
XLA Ops:
  22.3 167.3 %all-gather.9.cloned.1.call-done = bf16[1,1536,4608]{2,1,0:T(8,128)(2,1)} async-done(((bf16[1,48,4608]{2,1,0:T(8,128)(2,1)}), bf16[1,1536,4608]{2,1,0:T(8,128)(2,1)}) %all-gather.9.cloned.1.call-update) | async-done | bytes 14155792 | tf_op jit(solution)/shard_map/all_gather | solution.py:84
  189.6 7.3 fusion.169
  197.9 4.6 collective-permute-start.4
  206.1 8.1 collective-permute-start
  217.8 5.7 collective-permute-done.4
  224.4 7.2 collective-permute-done.5
  236.8 7.7 collective-permute-done.1
  248.7 11.6 %fusion.170 = (f32[24,256]{1,0:T(8,128)S(1)}, f32[24,256,768]{2,1,0:T(8,128)}) fusion(pred[256,768]{1,0:T(8,128)(4,1)} %get-tuple-element.183, bf16[256,24,64]{0,2,1:T(8,128)(2,1)} %bitcast.166, bf16[768,24,64]{0,2,1:T(8,128)(2,1)} %bitcast.162), kind=kOutput, calls=%fused_computation.313 | convolution fusion | flops 618136320 | bytes 22241280 | tf_op jit(solution)/shard_map/sub | solution.py:47
  260.4 9.0 %fusion.79 = bf16[24,64,256]{2,1,0:T(8,128)(2,1)S(1)} fusion(bf16[768,24,64]{0,2,1:T(8,128)(2,1)} %bitcast.164, f32[24,256,768]{2,1,0:T(8,128)} %get-tuple-element.173, f32[24,256]{1,0:T(8,128)S(1)} %get-tuple-element.172), kind=kOutput, calls=%fused_computation.140 | convolution fusion | flops 613810176 | bytes 22044672 | tf_op jit(solution)/shard_map/hqk,khd->qhd/dot_general | solution.py:49
  269.4 83.4 %all-gather.11.cloned.1.call-done = bf16[1,1536,1536]{2,1,0:T(8,128)(2,1)} async-done(((bf16[1,48,1536]{2,1,0:T(8,128)(2,1)}), bf16[1,1536,1536]{2,1,0:T(8,128)(2,1)}) %all-gather.11.cloned.1.call-update) | async-done | bytes 4718608 | tf_op jit(solution)/shard_map/all_gather | solution.py:85
  356.9 166.5 %all-gather.13.cloned.1.call-done = bf16[1,1536,3072]{2,1,0:T(8,128)(2,1)} async-done(((bf16[1,48,3072]{2,1,0:T(8,128)(2,1)}), bf16[1,1536,3072]{2,1,0:T(8,128)(2,1)}) %all-gather.13.cloned.1.call-update) | async-done | bytes 9437200 | tf_op jit(solution)/shard_map/all_gather | solution.py:86
  523.4 5.2 fusion.14
  536.3 148.1 %all-gather.15.cloned.1.call-done = bf16[1,1536,1536]{2,1,0:T(8,128)(2,1)} async-done(((bf16[1,48,1536]{2,1,0:T(8,128)(2,1)}), bf16[1,1536,1536]{2,1,0:T(8,128)(2,1)}) %all-gather.15.cloned.1.call-update) | async-done | bytes 4718608 | tf_op jit(solution)/shard_map/all_gather | solution.py:87
  685.1 21.7 %fusion.45 = bf16[256,1536]{1,0:T(8,128)(2,1)S(1)} fusion(f32[256,1536]{1,0:T(8,128)S(1)} %get-tuple-element.175, bf16[1,1536,1536]{2,1,0:T(8,128)(2,1)} %all-gather.15.cloned.1.call-done, bf16[256,1536]{1,0:T(8,128)(2,1)S(1)} %fusion.76, bf16[15,1536]{1,0:T(8,128)(2,1)} %copy-done.59, bf16[15,1536]{1,0:T(8,128)(2,1)} %copy-done.58, ...), kind=kOutput, calls=%fused_computation.93 | convolution fusion | flops 1294073856 | bytes 8154624 | tf_op jit(solution)/shard_map/dot_general | solution.py:122
  708.9 12.7 %collective-permute-done.8 = bf16[256,1536]{1,0:T(8,128)(2,1)S(1)} collective-permute-done((bf16[256,1536]{1,0:T(8,128)(2,1)S(1)}, bf16[256,1536]{1,0:T(8,128)(2,1)S(1)}, u32[]{:S(2)}, u32[]{:S(2)}) %collective-permute-start.8) | collective-permute-done | bytes 786464 | tf_op jit(solution)/shard_map/ppermute | solution.py:27
  723.5 7.3 fusion.172
  740.4 8.1 collective-permute-start.9
  751.8 5.8 collective-permute-done.12
  761.9 4.2 collective-permute-done.10
  770.3 11.7 %fusion.173 = (f32[24,256]{1,0:T(8,128)S(1)}, f32[24,256,768]{2,1,0:T(8,128)}) fusion(pred[256,768]{1,0:T(8,128)(4,1)S(1)} %get-tuple-element.182, bf16[256,24,64]{0,2,1:T(8,128)(2,1)} %bitcast.165, bf16[768,24,64]{0,2,1:T(8,128)(2,1)} %bitcast.161), kind=kOutput, calls=%fused_computation.316 | convolution fusion | flops 618136320 | bytes 22241280 | tf_op jit(solution)/shard_map/sub | solution.py:47
  782.0 9.1 %fusion.78 = bf16[24,64,256]{2,1,0:T(8,128)(2,1)S(1)} fusion(bf16[768,24,64]{0,2,1:T(8,128)(2,1)} %bitcast.163, f32[24,256,768]{2,1,0:T(8,128)} %get-tuple-element.179, f32[24,256]{1,0:T(8,128)S(1)} %get-tuple-element.178), kind=kOutput, calls=%fused_computation.139 | convolution fusion | flops 613810176 | bytes 22044672 | tf_op jit(solution)/shard_map/hqk,khd->qhd/dot_general | solution.py:49
  793.0 5.4 fusion.12
  805.4 7.4 collective-permute-done.14
  813.1 12.4 %fusion.48 = bf16[1,256,1536]{2,1,0:T(8,128)(2,1)S(1)} fusion(f32[256,1536]{1,0:T(8,128)S(1)} %get-tuple-element.181, bf16[1,1536,1536]{2,1,0:T(8,128)(2,1)S(1)} %bitcast.235, bf16[256,1536]{1,0:T(8,128)(2,1)S(1)} %fusion.77, bf16[15,1536]{1,0:T(8,128)(2,1)S(1)} %collective-permute-done.14, bf16[15,1536]{1,0:T(8,128)(2,1)S(1)} %collective-permute-done.13, ...), kind=kOutput, calls=%fused_computation.94 | convolution fusion | flops 1294073856 | bytes 8154624 | tf_op jit(solution)/shard_map/dot_general | solution.py:122
  (208 shorter events, 81.3 us)
Async XLA Ops:
  6.5 183.1 %all-gather.9.cloned.1.call-start = ((), (), s32[]{:S(2)}) async-start(), calls=%async_computation | async-start | bytes 14598144 | tf_op jit(solution)/shard_map/all_gather | solution.py:84
  7.3 345.5 %all-gather.11.cloned.1.call-start = ((), (), s32[]{:S(2)}) async-start(), calls=%async_computation.1 | async-start | bytes 4866048 | tf_op jit(solution)/shard_map/all_gather | solution.py:85
  8.0 515.3 %all-gather.13.cloned.1.call-start = ((), (), s32[]{:S(2)}) async-start(), calls=%async_computation.2 | async-start | bytes 9732096 | tf_op jit(solution)/shard_map/all_gather | solution.py:86
  8.8 675.7 %all-gather.15.cloned.1.call-start = ((), (), s32[]{:S(2)}) async-start(), calls=%async_computation.3 | async-start | bytes 4866048 | tf_op jit(solution)/shard_map/all_gather | solution.py:87
  9.5 7.6 collective-permute-start.2
  11.4 9.8 %collective-permute-start.3 = (s32[5,256]{1,0:T(8,128)S(1)}, s32[5,256]{1,0:T(8,128)S(1)}, u32[]{:S(2)}, u32[]{:S(2)}) collective-permute-start(s32[5,256]{1,0:T(8,128)S(1)} %broadcast_add_fusion), channel_id=1, source_target_pairs={{1,0},{2,1},{3,2},{4,3},{5,4},{6,5},{7,6},{8,7},{9,8},{10,9},{11,1... | collective-permute-start | bytes 15368 | tf_op jit(solution)/shard_map/ppermute | solution.py:19
  197.9 25.6 %copy-start.2 = (bf16[256,1536]{1,0:T(8,128)(2,1)}, bf16[256,1536]{1,0:T(8,128)(2,1)S(1)}, u32[]{:S(2)}) copy-start(bf16[256,1536]{1,0:T(8,128)(2,1)S(1)} %get-tuple-element.42) | copy-start | bytes 2359300
  197.9 25.6 %collective-permute-start.4 = (bf16[256,1536]{1,0:T(8,128)(2,1)S(1)}, bf16[256,1536]{1,0:T(8,128)(2,1)S(1)}, u32[]{:S(2)}, u32[]{:S(2)}) collective-permute-start(bf16[256,1536]{1,0:T(8,128)(2,1)S(1)} %get-tuple-element.42), channel_id=1, source_target_pairs={{0,1},{1,2},{2,3},{3,4},{4,5},{5,6},{6,7},{7,8},{8,9},{9,10},{10,1... | collective-permute-start | bytes 2359304 | tf_op jit(solution)/shard_map/ppermute | solution.py:16
  202.5 29.1 %collective-permute-start.5 = (bf16[256,1536]{1,0:T(8,128)(2,1)S(1)}, bf16[256,1536]{1,0:T(8,128)(2,1)}, u32[]{:S(2)}, u32[]{:S(2)}) collective-permute-start(bf16[256,1536]{1,0:T(8,128)(2,1)S(1)} %get-tuple-element.42), channel_id=1, source_target_pairs={{1,0},{2,1},{3,2},{4,3},{5,4},{6,5},{7,6},{8,7},{9,8},{10,9},{11,1... | collective-permute-start | bytes 2359304 | tf_op jit(solution)/shard_map/ppermute | solution.py:19
  206.1 30.7 %collective-permute-start = (bf16[256,1536]{1,0:T(8,128)(2,1)}, bf16[256,1536]{1,0:T(8,128)(2,1)}, u32[]{:S(2)}, u32[]{:S(2)}) collective-permute-start(bf16[256,1536]{1,0:T(8,128)(2,1)} %get-tuple-element.43), channel_id=1, source_target_pairs={{0,1},{1,2},{2,3},{3,4},{4,5},{5,6},{6,7},{7,8},{8,9},{9,10},{10,1... | collective-permute-start | bytes 2359304 | tf_op jit(solution)/shard_map/ppermute | solution.py:16
  214.2 30.3 %collective-permute-start.1 = (bf16[256,1536]{1,0:T(8,128)(2,1)}, bf16[256,1536]{1,0:T(8,128)(2,1)}, u32[]{:S(2)}, u32[]{:S(2)}) collective-permute-start(bf16[256,1536]{1,0:T(8,128)(2,1)} %get-tuple-element.43), channel_id=1, source_target_pairs={{1,0},{2,1},{3,2},{4,3},{5,4},{6,5},{7,6},{8,7},{9,8},{10,9},{11,1... | collective-permute-start | bytes 2359304 | tf_op jit(solution)/shard_map/ppermute | solution.py:19
  529.2 155.3 %collective-permute-start.6 = (bf16[15,1536]{1,0:T(8,128)(2,1)S(1)}, bf16[15,1536]{1,0:T(8,128)(2,1)S(1)}, u32[]{:S(2)}, u32[]{:S(2)}) collective-permute-start(bf16[15,1536]{1,0:T(8,128)(2,1)S(1)} %get-tuple-element.46), channel_id=1, source_target_pairs={{0,1},{1,2},{2,3},{3,4},{4,5},{5,6},{6,7},{7,8},{8,9},{9,10},{10,1... | collective-permute-start | bytes 138248 | tf_op jit(solution)/shard_map/ppermute | solution.py:16
  532.8 151.7 %collective-permute-start.7 = (bf16[15,1536]{1,0:T(8,128)(2,1)S(1)}, bf16[15,1536]{1,0:T(8,128)(2,1)S(1)}, u32[]{:S(2)}, u32[]{:S(2)}) collective-permute-start(bf16[15,1536]{1,0:T(8,128)(2,1)S(1)} %get-tuple-element.47), channel_id=1, source_target_pairs={{1,0},{2,1},{3,2},{4,3},{5,4},{6,5},{7,6},{8,7},{9,8},{10,9},{11,1... | collective-permute-start | bytes 138248 | tf_op jit(solution)/shard_map/ppermute | solution.py:19
  706.8 14.8 %collective-permute-start.8 = (bf16[256,1536]{1,0:T(8,128)(2,1)S(1)}, bf16[256,1536]{1,0:T(8,128)(2,1)S(1)}, u32[]{:S(2)}, u32[]{:S(2)}) collective-permute-start(bf16[256,1536]{1,0:T(8,128)(2,1)S(1)} %fusion.45), channel_id=1, source_target_pairs={{0,32},{32,64},{64,96},{1,33},{33,65},{65,97},{2,34},{34,66},{66,9... | collective-permute-start | bytes 2359304 | tf_op jit(solution)/shard_map/ppermute | solution.py:27
  731.8 19.1 %copy-start.1 = (bf16[256,1536]{1,0:T(8,128)(2,1)}, bf16[256,1536]{1,0:T(8,128)(2,1)S(1)}, u32[]{:S(2)}) copy-start(bf16[256,1536]{1,0:T(8,128)(2,1)S(1)} %get-tuple-element.40) | copy-start | bytes 2359300
  731.8 19.1 %collective-permute-start.11 = (bf16[256,1536]{1,0:T(8,128)(2,1)S(1)}, bf16[256,1536]{1,0:T(8,128)(2,1)S(1)}, u32[]{:S(2)}, u32[]{:S(2)}) collective-permute-start(bf16[256,1536]{1,0:T(8,128)(2,1)S(1)} %get-tuple-element.40), channel_id=1, source_target_pairs={{0,1},{1,2},{2,3},{3,4},{4,5},{5,6},{6,7},{7,8},{8,9},{9,10},{10,1... | collective-permute-start | bytes 2359304 | tf_op jit(solution)/shard_map/ppermute | solution.py:16
  734.4 23.2 %collective-permute-start.12 = (bf16[256,1536]{1,0:T(8,128)(2,1)S(1)}, bf16[256,1536]{1,0:T(8,128)(2,1)}, u32[]{:S(2)}, u32[]{:S(2)}) collective-permute-start(bf16[256,1536]{1,0:T(8,128)(2,1)S(1)} %get-tuple-element.40), channel_id=1, source_target_pairs={{1,0},{2,1},{3,2},{4,3},{5,4},{6,5},{7,6},{8,7},{9,8},{10,9},{11,1... | collective-permute-start | bytes 2359304 | tf_op jit(solution)/shard_map/ppermute | solution.py:19
  738.5 27.6 %collective-permute-start.10 = (bf16[256,1536]{1,0:T(8,128)(2,1)}, bf16[256,1536]{1,0:T(8,128)(2,1)}, u32[]{:S(2)}, u32[]{:S(2)}) collective-permute-start(bf16[256,1536]{1,0:T(8,128)(2,1)} %get-tuple-element.41), channel_id=1, source_target_pairs={{1,0},{2,1},{3,2},{4,3},{5,4},{6,5},{7,6},{8,7},{9,8},{10,9},{11,1... | collective-permute-start | bytes 2359304 | tf_op jit(solution)/shard_map/ppermute | solution.py:19
  740.4 25.6 %collective-permute-start.9 = (bf16[256,1536]{1,0:T(8,128)(2,1)}, bf16[256,1536]{1,0:T(8,128)(2,1)}, u32[]{:S(2)}, u32[]{:S(2)}) collective-permute-start(bf16[256,1536]{1,0:T(8,128)(2,1)} %get-tuple-element.41), channel_id=1, source_target_pairs={{0,1},{1,2},{2,3},{3,4},{4,5},{5,6},{6,7},{7,8},{8,9},{9,10},{10,1... | collective-permute-start | bytes 2359304 | tf_op jit(solution)/shard_map/ppermute | solution.py:16
  770.3 20.8 %slice-start = ((s8[4718592]{0:T(1024)(128)(4,1)}), s8[524288]{0:T(1024)(128)(4,1)S(1)}, s32[]{:S(2)}) async-start(s8[4718592]{0:T(1024)(128)(4,1)} %bitcast.157), calls=%async_computation.4 | async-start | bytes 1048576
  791.1 21.7 %slice-start.2 = ((s8[4718592]{0:T(1024)(128)(4,1)}), s8[524288]{0:T(1024)(128)(4,1)S(1)}, s32[]{:S(2)}) async-start(s8[4718592]{0:T(1024)(128)(4,1)} %bitcast.234), calls=%async_computation.6 | async-start | bytes 1048576
  793.0 19.9 %slice-start.3 = ((s8[4718592]{0:T(1024)(128)(4,1)}), s8[4194304]{0:T(1024)(128)(4,1)S(1)}, s32[]{:S(2)}) async-start(s8[4718592]{0:T(1024)(128)(4,1)} %bitcast.234), calls=%async_computation.7 | async-start | bytes 8388608
  799.2 6.2 collective-permute-start.13
  802.6 10.2 %collective-permute-start.14 = (bf16[15,1536]{1,0:T(8,128)(2,1)S(1)}, bf16[15,1536]{1,0:T(8,128)(2,1)S(1)}, u32[]{:S(2)}, u32[]{:S(2)}) collective-permute-start(bf16[15,1536]{1,0:T(8,128)(2,1)S(1)} %get-tuple-element.45), channel_id=1, source_target_pairs={{1,0},{2,1},{3,2},{4,3},{5,4},{6,5},{7,6},{8,7},{9,8},{10,9},{11,1... | collective-permute-start | bytes 138248 | tf_op jit(solution)/shard_map/ppermute | solution.py:19
  (59 other events, 568.4 us)
Sparse Core Ops, SparseCore 0:
  9.0 180.5 all-gather.8
  191.2 161.4 all-gather.10
  354.4 168.9 all-gather.12
  524.9 159.5 all-gather.14
where the time goes:
time: 838 us; the launch traced here: 834 us
  waiting for transfers between devices  624 us (74%)
  matrix products  106 us (13%)
  starting transfers between devices  53.3 us (6%)
  local copies, waits for them, and re-layouts  19.3 us (2%)
  other arithmetic  16.1 us (2%)
  between operations  14.6 us (2%)
    all_gather x1, waiting for transfers between devices, on_device(): lax.all_gather(triple_projection_matrix[0], 'frame', axis=0, tiled=True)  167 us
    all_gather x1, waiting for transfers between devices, on_device(): lax.all_gather(sigmoid_expand_matrix[0], 'frame', axis=0, tiled=True)  166 us
    all_gather x1, waiting for transfers between devices, on_device(): lax.all_gather(combine_channel_matrix[0], 'frame', axis=0, tiled=True)  148 us
    all_gather x1, waiting for transfers between devices, on_device(): lax.all_gather(selfattend_final_matrix[0], 'frame', axis=0, tiled=True)  83.4 us
    ppermute x7, waiting for transfers between devices, extended(): lax.ppermute(lax.slice_in_dim(block, 0, width, axis=dim), axis, backward)  36.4 us
    dot_general x2, matrix products, on_device(): resid = resid + jnp.dot(act, full_mix, preferred_element_type=jnp.float32)  34.1 us
    ppermute x7, starting transfers between devices, extended(): lax.ppermute(lax.slice_in_dim(block, block.shape[dim] - width, None, axis...  32.5 us
    sub x2, matrix products, attend(): expd = jnp.exp(scores - top)  23.3 us
  transfers between devices with their start and end apart: 19, of which 14 were waited for; matrix products, arithmetic and copies ran while one was open for 7% of the time, Pallas kernels for 0%

commit v1 on v0

--- a/solution.py
+++ b/solution.py
@@ -82,7 +82,15 @@
     seg_all = extended(speaker_clip_ids + 1, (("frame", 1),), sample_lines)
     full_qkv, full_out, full_glu, full_mix = (
         lax.all_gather(triple_projection_matrix[0], "frame", axis=0, tiled=True),
-        lax.all_gather(selfattend_final_matrix[0], "frame", axis=0, tiled=True),
+        jnp.concatenate(
+            lax.all_to_all(
+                jnp.stack(lax.psum(1, axis_name="frame") * [selfattend_final_matrix[0]]),
+                axis_name="frame",
+                split_axis=0,
+                concat_axis=0,
+            ),
+            axis=0,
+        ),
         lax.all_gather(sigmoid_expand_matrix[0], "frame", axis=0, tiled=True),
         lax.all_gather(combine_channel_matrix[0], "frame", axis=0, tiled=True),
     )

time: 838 us -> 748 us (0.89)
  waiting for transfers between devices: 624 us -> 519 us
    all_gather x1, waiting for transfers between devices: 166 us -> 73.9 us  [on_device(): lax.all_gather(sigmoid_expand_matrix[0], 'frame', axis=0, tiled=True)]
    all_gather x1 -> x0, waiting for transfers between devices: 83.4 us -> none  [on_device(): lax.all_gather(selfattend_final_matrix[0], 'frame', axis=0, tiled=True)]
    all_gather x1, waiting for transfers between devices: 167 us -> 220 us  [on_device(): lax.all_gather(triple_projection_matrix[0], 'frame', axis=0, tiled=True)]
    ppermute x7, waiting for transfers between devices: 7.82 us -> 27.4 us  [extended(): lax.ppermute(lax.slice_in_dim(block, block.shape[dim] - width, None, axis...]
  transfers between devices with their start and end apart: 19 -> 19, of which waited for: 14 -> 12; matrix products, arithmetic and copies ran while one was open for 7% -> 9% of each run, Pallas kernels for 0% -> 0%
where the time goes in v1:
time: 748 us; the launch traced here: 743 us
  waiting for transfers between devices  519 us (69%)
  matrix products  109 us (15%)
  starting transfers between devices  61.4 us (8%)
  local copies, waits for them, and re-layouts  22.9 us (3%)
  other arithmetic  16.1 us (2%)
  between operations  14.7 us (2%)
    all_gather x1, waiting for transfers between devices, on_device(): lax.all_gather(triple_projection_matrix[0], 'frame', axis=0, tiled=True)  220 us
    all_gather x1, waiting for transfers between devices, on_device(): lax.all_gather(combine_channel_matrix[0], 'frame', axis=0, tiled=True)  148 us
    all_gather x1, waiting for transfers between devices, on_device(): lax.all_gather(sigmoid_expand_matrix[0], 'frame', axis=0, tiled=True)  73.9 us
    dot_general x2, matrix products, on_device(): resid = resid + jnp.dot(act, full_mix, preferred_element_type=jnp.float32)  34.9 us
    ppermute x7, waiting for transfers between devices, extended(): lax.ppermute(lax.slice_in_dim(block, 0, width, axis=dim), axis, backward)  34.6 us
    ppermute x7, starting transfers between devices, extended(): lax.ppermute(lax.slice_in_dim(block, block.shape[dim] - width, None, axis...  33.4 us
    ppermute x7, waiting for transfers between devices, extended(): lax.ppermute(lax.slice_in_dim(block, block.shape[dim] - width, None, axis...  27.4 us
    sub x2, matrix products, attend(): expd = jnp.exp(scores - top)  24 us
  transfers between devices with their start and end apart: 19, of which 12 were waited for; matrix products, arithmetic and copies ran while one was open for 9% of the time, Pallas kernels for 0%

profile of v1, /device:TPU:118, one launch (start us, length us, event | category | flops | bytes accessed | tf_op | source)
XLA Modules:
  0.0 742.8 jit_solution(9613991202187113826)
XLA Ops:
  18.1 7.9 %all-to-all-start = ((bf16[32,48,1536]{2,1,0:T(8,128)(2,1)}), bf16[32,48,1536]{2,1,0:T(8,128)(2,1)}, u32[]{:S(2)}, u32[]{:S(2)}) async-start(bf16[32,48,1536]{2,1,0:T(8,128)(2,1)} %stack.12), calls=%async_computation | async-start | bytes 9437184 | tf_op jit(solution)/shard_map/all_to_all | solution.py:86
  29.7 220.2 %all-gather.7.cloned.1.call-done = bf16[1,1536,4608]{2,1,0:T(8,128)(2,1)} async-done(((bf16[1,48,4608]{2,1,0:T(8,128)(2,1)}), bf16[1,1536,4608]{2,1,0:T(8,128)(2,1)}) %all-gather.7.cloned.1.call-update) | async-done | bytes 14155792 | tf_op jit(solution)/shard_map/all_gather | solution.py:84
  249.9 7.3 fusion.159
  258.2 4.9 collective-permute-start.4
  266.7 8.1 %collective-permute-start = (bf16[256,1536]{1,0:T(8,128)(2,1)}, bf16[256,1536]{1,0:T(8,128)(2,1)}, u32[]{:S(2)}, u32[]{:S(2)}) collective-permute-start(bf16[256,1536]{1,0:T(8,128)(2,1)} %get-tuple-element.43), channel_id=1, source_target_pairs={{0,1},{1,2},{2,3},{3,4},{4,5},{5,6},{6,7},{7,8},{8,9},{9,10},{10,1... | collective-permute-start | bytes 2359304 | tf_op jit(solution)/shard_map/ppermute | solution.py:16
  278.5 18.4 %collective-permute-done.4 = bf16[256,1536]{1,0:T(8,128)(2,1)S(1)} collective-permute-done((bf16[256,1536]{1,0:T(8,128)(2,1)S(1)}, bf16[256,1536]{1,0:T(8,128)(2,1)S(1)}, u32[]{:S(2)}, u32[]{:S(2)}) %collective-permute-start.4) | collective-permute-done | bytes 786464 | tf_op jit(solution)/shard_map/ppermute | solution.py:16
  297.7 7.8 %collective-permute-done.5 = bf16[256,1536]{1,0:T(8,128)(2,1)} collective-permute-done((bf16[256,1536]{1,0:T(8,128)(2,1)S(1)}, bf16[256,1536]{1,0:T(8,128)(2,1)}, u32[]{:S(2)}, u32[]{:S(2)}) %collective-permute-start.5) | collective-permute-done | bytes 786464 | tf_op jit(solution)/shard_map/ppermute | solution.py:19
  309.9 8.0 %collective-permute-done = bf16[256,1536]{1,0:T(8,128)(2,1)} collective-permute-done((bf16[256,1536]{1,0:T(8,128)(2,1)}, bf16[256,1536]{1,0:T(8,128)(2,1)}, u32[]{:S(2)}, u32[]{:S(2)}) %collective-permute-start) | collective-permute-done | bytes 786464 | tf_op jit(solution)/shard_map/ppermute | solution.py:16
  317.9 9.2 %collective-permute-done.1 = bf16[256,1536]{1,0:T(8,128)(2,1)} collective-permute-done((bf16[256,1536]{1,0:T(8,128)(2,1)}, bf16[256,1536]{1,0:T(8,128)(2,1)}, u32[]{:S(2)}, u32[]{:S(2)}) %collective-permute-start.1) | collective-permute-done | bytes 786464 | tf_op jit(solution)/shard_map/ppermute | solution.py:19
  331.3 11.6 %fusion.160 = (f32[24,256]{1,0:T(8,128)S(1)}, f32[24,256,768]{2,1,0:T(8,128)}) fusion(pred[256,768]{1,0:T(8,128)(4,1)} %get-tuple-element.183, bf16[256,24,64]{0,2,1:T(8,128)(2,1)} %bitcast.155, bf16[768,24,64]{0,2,1:T(8,128)(2,1)} %bitcast.151), kind=kOutput, calls=%fused_computation.309 | convolution fusion | flops 618136320 | bytes 22241280 | tf_op jit(solution)/shard_map/sub | solution.py:47
  342.9 9.1 %fusion.69 = bf16[24,64,256]{2,1,0:T(8,128)(2,1)S(1)} fusion(bf16[768,24,64]{0,2,1:T(8,128)(2,1)} %bitcast.153, f32[24,256,768]{2,1,0:T(8,128)} %get-tuple-element.173, f32[24,256]{1,0:T(8,128)S(1)} %get-tuple-element.172), kind=kOutput, calls=%fused_computation.136 | convolution fusion | flops 613810176 | bytes 22044672 | tf_op jit(solution)/shard_map/hqk,khd->qhd/dot_general | solution.py:49
  356.2 73.9 %all-gather.9.cloned.1.call-done = bf16[1,1536,3072]{2,1,0:T(8,128)(2,1)} async-done(((bf16[1,48,3072]{2,1,0:T(8,128)(2,1)}), bf16[1,1536,3072]{2,1,0:T(8,128)(2,1)}) %all-gather.9.cloned.1.call-update) | async-done | bytes 9437200 | tf_op jit(solution)/shard_map/all_gather | solution.py:94
  430.0 5.2 fusion.14
  442.7 147.6 %all-gather.11.cloned.1.call-done = bf16[1,1536,1536]{2,1,0:T(8,128)(2,1)} async-done(((bf16[1,48,1536]{2,1,0:T(8,128)(2,1)}), bf16[1,1536,1536]{2,1,0:T(8,128)(2,1)}) %all-gather.11.cloned.1.call-update) | async-done | bytes 4718608 | tf_op jit(solution)/shard_map/all_gather | solution.py:95
  590.9 22.5 %fusion.35 = bf16[256,1536]{1,0:T(8,128)(2,1)} fusion(f32[256,1536]{1,0:T(8,128)S(1)} %get-tuple-element.175, bf16[1,1536,1536]{2,1,0:T(8,128)(2,1)} %all-gather.11.cloned.1.call-done, bf16[256,1536]{1,0:T(8,128)(2,1)S(1)} %fusion.66, bf16[15,1536]{1,0:T(8,128)(2,1)} %copy-done.59, bf16[15,1536]{1,0:T(8,128)(2,1)} %copy-done.58, ...), kind=kOutput, calls=%fused_computation.89 | convolution fusion | flops 1294073856 | bytes 8154624 | tf_op jit(solution)/shard_map/dot_general | solution.py:130
  615.5 12.9 %collective-permute-done.8 = bf16[256,1536]{1,0:T(8,128)(2,1)S(1)} collective-permute-done((bf16[256,1536]{1,0:T(8,128)(2,1)}, bf16[256,1536]{1,0:T(8,128)(2,1)S(1)}, u32[]{:S(2)}, u32[]{:S(2)}) %collective-permute-start.8) | collective-permute-done | bytes 786464 | tf_op jit(solution)/shard_map/ppermute | solution.py:27
  629.1 7.3 fusion.162
  646.1 8.1 %collective-permute-start.9 = (bf16[256,1536]{1,0:T(8,128)(2,1)}, bf16[256,1536]{1,0:T(8,128)(2,1)}, u32[]{:S(2)}, u32[]{:S(2)}) collective-permute-start(bf16[256,1536]{1,0:T(8,128)(2,1)} %get-tuple-element.41), channel_id=1, source_target_pairs={{0,1},{1,2},{2,3},{3,4},{4,5},{5,6},{6,7},{7,8},{8,9},{9,10},{10,1... | collective-permute-start | bytes 2359304 | tf_op jit(solution)/shard_map/ppermute | solution.py:16
  657.4 6.1 collective-permute-done.12
  676.2 12.3 %fusion.163 = (f32[24,256]{1,0:T(8,128)}, f32[24,256,768]{2,1,0:T(8,128)}) fusion(pred[256,768]{1,0:T(8,128)(4,1)S(1)} %get-tuple-element.182, bf16[256,24,64]{0,2,1:T(8,128)(2,1)} %bitcast.154, bf16[768,24,64]{0,2,1:T(8,128)(2,1)} %bitcast.150), kind=kOutput, calls=%fused_computation.312 | convolution fusion | flops 618136320 | bytes 22241280 | tf_op jit(solution)/shard_map/sub | solution.py:47
  688.5 8.0 %fusion.68 = bf16[24,64,256]{2,1,0:T(8,128)(2,1)S(1)} fusion(bf16[768,24,64]{0,2,1:T(8,128)(2,1)S(1)} %bitcast.152, f32[24,256,768]{2,1,0:T(8,128)} %get-tuple-element.179, f32[24,256]{1,0:T(8,128)} %get-tuple-element.178), kind=kOutput, calls=%fused_computation.135 | convolution fusion | flops 613810176 | bytes 22044672 | tf_op jit(solution)/shard_map/hqk,khd->qhd/dot_general | solution.py:49
  700.8 5.5 fusion.12
  713.4 7.4 collective-permute-done.14
  721.0 12.4 %fusion.38 = bf16[1,256,1536]{2,1,0:T(8,128)(2,1)S(1)} fusion(f32[256,1536]{1,0:T(8,128)S(1)} %get-tuple-element.181, bf16[1,1536,1536]{2,1,0:T(8,128)(2,1)S(1)} %bitcast.224, bf16[256,1536]{1,0:T(8,128)(2,1)S(1)} %fusion.67, bf16[15,1536]{1,0:T(8,128)(2,1)S(1)} %collective-permute-done.14, bf16[15,1536]{1,0:T(8,128)(2,1)S(1)} %collective-permute-done.13, ...), kind=kOutput, calls=%fused_computation.90 | convolution fusion | flops 1294073856 | bytes 8154624 | tf_op jit(solution)/shard_map/dot_general | solution.py:130
  (203 shorter events, 86.3 us)
Async XLA Ops:
  6.5 243.4 %all-gather.7.cloned.1.call-start = ((), (), s32[]{:S(2)}) async-start(), calls=%async_computation.1 | async-start | bytes 14598144 | tf_op jit(solution)/shard_map/all_gather | solution.py:84
  7.3 422.8 %all-gather.9.cloned.1.call-start = ((), (), s32[]{:S(2)}) async-start(), calls=%async_computation.2 | async-start | bytes 9732096 | tf_op jit(solution)/shard_map/all_gather | solution.py:94
  8.7 19.9 %collective-permute-start.2 = (s32[5,256]{1,0:T(8,128)S(1)}, s32[5,256]{1,0:T(8,128)S(1)}, u32[]{:S(2)}, u32[]{:S(2)}) collective-permute-start(s32[5,256]{1,0:T(8,128)S(1)} %broadcast_add_fusion), channel_id=1, source_target_pairs={{0,1},{1,2},{2,3},{3,4},{4,5},{5,6},{6,7},{7,8},{8,9},{9,10},{10,1... | collective-permute-start | bytes 15368 | tf_op jit(solution)/shard_map/ppermute | solution.py:16
  10.6 18.0 %collective-permute-start.3 = (s32[5,256]{1,0:T(8,128)S(1)}, s32[5,256]{1,0:T(8,128)S(1)}, u32[]{:S(2)}, u32[]{:S(2)}) collective-permute-start(s32[5,256]{1,0:T(8,128)S(1)} %broadcast_add_fusion), channel_id=1, source_target_pairs={{1,0},{2,1},{3,2},{4,3},{5,4},{6,5},{7,6},{8,7},{9,8},{10,9},{11,1... | collective-permute-start | bytes 15368 | tf_op jit(solution)/shard_map/ppermute | solution.py:19
  18.1 333.9 %all-to-all-start = ((bf16[32,48,1536]{2,1,0:T(8,128)(2,1)}), bf16[32,48,1536]{2,1,0:T(8,128)(2,1)}, u32[]{:S(2)}, u32[]{:S(2)}) async-start(bf16[32,48,1536]{2,1,0:T(8,128)(2,1)} %stack.12), calls=%async_computation | async-start | bytes 9437184 | tf_op jit(solution)/shard_map/all_to_all | solution.py:86
  26.1 564.2 %all-gather.11.cloned.1.call-start = ((), (), s32[]{:S(2)}) async-start(), calls=%async_computation.3 | async-start | bytes 4866048 | tf_op jit(solution)/shard_map/all_gather | solution.py:95
  258.2 20.3 %copy-start.2 = (bf16[256,1536]{1,0:T(8,128)(2,1)}, bf16[256,1536]{1,0:T(8,128)(2,1)S(1)}, u32[]{:S(2)}) copy-start(bf16[256,1536]{1,0:T(8,128)(2,1)S(1)} %get-tuple-element.42) | copy-start | bytes 2359300
  258.2 38.7 %collective-permute-start.4 = (bf16[256,1536]{1,0:T(8,128)(2,1)S(1)}, bf16[256,1536]{1,0:T(8,128)(2,1)S(1)}, u32[]{:S(2)}, u32[]{:S(2)}) collective-permute-start(bf16[256,1536]{1,0:T(8,128)(2,1)S(1)} %get-tuple-element.42), channel_id=1, source_target_pairs={{0,1},{1,2},{2,3},{3,4},{4,5},{5,6},{6,7},{7,8},{8,9},{9,10},{10,1... | collective-permute-start | bytes 2359304 | tf_op jit(solution)/shard_map/ppermute | solution.py:16
  263.1 42.5 %collective-permute-start.5 = (bf16[256,1536]{1,0:T(8,128)(2,1)S(1)}, bf16[256,1536]{1,0:T(8,128)(2,1)}, u32[]{:S(2)}, u32[]{:S(2)}) collective-permute-start(bf16[256,1536]{1,0:T(8,128)(2,1)S(1)} %get-tuple-element.42), channel_id=1, source_target_pairs={{1,0},{2,1},{3,2},{4,3},{5,4},{6,5},{7,6},{8,7},{9,8},{10,9},{11,1... | collective-permute-start | bytes 2359304 | tf_op jit(solution)/shard_map/ppermute | solution.py:19
  266.7 51.2 %collective-permute-start = (bf16[256,1536]{1,0:T(8,128)(2,1)}, bf16[256,1536]{1,0:T(8,128)(2,1)}, u32[]{:S(2)}, u32[]{:S(2)}) collective-permute-start(bf16[256,1536]{1,0:T(8,128)(2,1)} %get-tuple-element.43), channel_id=1, source_target_pairs={{0,1},{1,2},{2,3},{3,4},{4,5},{5,6},{6,7},{7,8},{8,9},{9,10},{10,1... | collective-permute-start | bytes 2359304 | tf_op jit(solution)/shard_map/ppermute | solution.py:16
  274.8 52.2 %collective-permute-start.1 = (bf16[256,1536]{1,0:T(8,128)(2,1)}, bf16[256,1536]{1,0:T(8,128)(2,1)}, u32[]{:S(2)}, u32[]{:S(2)}) collective-permute-start(bf16[256,1536]{1,0:T(8,128)(2,1)} %get-tuple-element.43), channel_id=1, source_target_pairs={{1,0},{2,1},{3,2},{4,3},{5,4},{6,5},{7,6},{8,7},{9,8},{10,9},{11,1... | collective-permute-start | bytes 2359304 | tf_op jit(solution)/shard_map/ppermute | solution.py:19
  435.8 154.4 %collective-permute-start.6 = (bf16[15,1536]{1,0:T(8,128)(2,1)S(1)}, bf16[15,1536]{1,0:T(8,128)(2,1)S(1)}, u32[]{:S(2)}, u32[]{:S(2)}) collective-permute-start(bf16[15,1536]{1,0:T(8,128)(2,1)S(1)} %get-tuple-element.46), channel_id=1, source_target_pairs={{0,1},{1,2},{2,3},{3,4},{4,5},{5,6},{6,7},{7,8},{8,9},{9,10},{10,1... | collective-permute-start | bytes 138248 | tf_op jit(solution)/shard_map/ppermute | solution.py:16
  439.8 150.5 %collective-permute-start.7 = (bf16[15,1536]{1,0:T(8,128)(2,1)S(1)}, bf16[15,1536]{1,0:T(8,128)(2,1)S(1)}, u32[]{:S(2)}, u32[]{:S(2)}) collective-permute-start(bf16[15,1536]{1,0:T(8,128)(2,1)S(1)} %get-tuple-element.47), channel_id=1, source_target_pairs={{1,0},{2,1},{3,2},{4,3},{5,4},{6,5},{7,6},{8,7},{9,8},{10,9},{11,1... | collective-permute-start | bytes 138248 | tf_op jit(solution)/shard_map/ppermute | solution.py:19
  590.9 37.5 %copy-start.6 = (bf16[1,256,1536]{2,1,0:T(8,128)(2,1)S(1)}, bf16[1,256,1536]{2,1,0:T(8,128)(2,1)}, u32[]{:S(2)}) copy-start(bf16[1,256,1536]{2,1,0:T(8,128)(2,1)} %param.10) | copy-start | bytes 2359300
  613.4 15.0 %collective-permute-start.8 = (bf16[256,1536]{1,0:T(8,128)(2,1)}, bf16[256,1536]{1,0:T(8,128)(2,1)S(1)}, u32[]{:S(2)}, u32[]{:S(2)}) collective-permute-start(bf16[256,1536]{1,0:T(8,128)(2,1)} %fusion.35), channel_id=1, source_target_pairs={{0,32},{32,64},{64,96},{1,33},{33,65},{65,97},{2,34},{34,66},{66,9... | collective-permute-start | bytes 2359304 | tf_op jit(solution)/shard_map/ppermute | solution.py:27
  637.4 18.1 %copy-start.1 = (bf16[256,1536]{1,0:T(8,128)(2,1)}, bf16[256,1536]{1,0:T(8,128)(2,1)S(1)}, u32[]{:S(2)}) copy-start(bf16[256,1536]{1,0:T(8,128)(2,1)S(1)} %get-tuple-element.40) | copy-start | bytes 2359300
  637.4 19.1 %collective-permute-start.11 = (bf16[256,1536]{1,0:T(8,128)(2,1)S(1)}, bf16[256,1536]{1,0:T(8,128)(2,1)S(1)}, u32[]{:S(2)}, u32[]{:S(2)}) collective-permute-start(bf16[256,1536]{1,0:T(8,128)(2,1)S(1)} %get-tuple-element.40), channel_id=1, source_target_pairs={{0,1},{1,2},{2,3},{3,4},{4,5},{5,6},{6,7},{7,8},{8,9},{9,10},{10,1... | collective-permute-start | bytes 2359304 | tf_op jit(solution)/shard_map/ppermute | solution.py:16
  640.3 23.2 %collective-permute-start.12 = (bf16[256,1536]{1,0:T(8,128)(2,1)S(1)}, bf16[256,1536]{1,0:T(8,128)(2,1)}, u32[]{:S(2)}, u32[]{:S(2)}) collective-permute-start(bf16[256,1536]{1,0:T(8,128)(2,1)S(1)} %get-tuple-element.40), channel_id=1, source_target_pairs={{1,0},{2,1},{3,2},{4,3},{5,4},{6,5},{7,6},{8,7},{9,8},{10,9},{11,1... | collective-permute-start | bytes 2359304 | tf_op jit(solution)/shard_map/ppermute | solution.py:19
  644.1 27.8 %collective-permute-start.10 = (bf16[256,1536]{1,0:T(8,128)(2,1)}, bf16[256,1536]{1,0:T(8,128)(2,1)}, u32[]{:S(2)}, u32[]{:S(2)}) collective-permute-start(bf16[256,1536]{1,0:T(8,128)(2,1)} %get-tuple-element.41), channel_id=1, source_target_pairs={{1,0},{2,1},{3,2},{4,3},{5,4},{6,5},{7,6},{8,7},{9,8},{10,9},{11,1... | collective-permute-start | bytes 2359304 | tf_op jit(solution)/shard_map/ppermute | solution.py:19
  646.1 25.9 %collective-permute-start.9 = (bf16[256,1536]{1,0:T(8,128)(2,1)}, bf16[256,1536]{1,0:T(8,128)(2,1)}, u32[]{:S(2)}, u32[]{:S(2)}) collective-permute-start(bf16[256,1536]{1,0:T(8,128)(2,1)} %get-tuple-element.41), channel_id=1, source_target_pairs={{0,1},{1,2},{2,3},{3,4},{4,5},{5,6},{6,7},{7,8},{8,9},{9,10},{10,1... | collective-permute-start | bytes 2359304 | tf_op jit(solution)/shard_map/ppermute | solution.py:16
  696.6 24.2 %slice-start = ((s8[4718592]{0:T(1024)(128)(4,1)}), s8[524288]{0:T(1024)(128)(4,1)S(1)}, s32[]{:S(2)}) async-start(s8[4718592]{0:T(1024)(128)(4,1)} %bitcast.223), calls=%async_computation.4 | async-start | bytes 1048576
  700.8 20.0 %slice-start.1 = ((s8[4718592]{0:T(1024)(128)(4,1)}), s8[4194304]{0:T(1024)(128)(4,1)S(1)}, s32[]{:S(2)}) async-start(s8[4718592]{0:T(1024)(128)(4,1)} %bitcast.223), calls=%async_computation.5 | async-start | bytes 8388608
  707.1 6.3 collective-permute-start.13
  710.5 10.2 %collective-permute-start.14 = (bf16[15,1536]{1,0:T(8,128)(2,1)S(1)}, bf16[15,1536]{1,0:T(8,128)(2,1)S(1)}, u32[]{:S(2)}, u32[]{:S(2)}) collective-permute-start(bf16[15,1536]{1,0:T(8,128)(2,1)S(1)} %get-tuple-element.45), channel_id=1, source_target_pairs={{1,0},{2,1},{3,2},{4,3},{5,4},{6,5},{7,6},{8,7},{9,8},{10,9},{11,1... | collective-permute-start | bytes 138248 | tf_op jit(solution)/shard_map/ppermute | solution.py:19
  (57 other events, 529.6 us)
Sparse Core Ops, SparseCore 0:
  9.0 240.8 all-gather.6
  251.6 178.4 all-gather.8
  431.7 158.5 all-gather.10
